TPU v7x, 32 devices: a whole 2x2x4 slice. The times are simulated.
32 devices in a mesh: pair: 8 (over y, x, core), row: 4 (over z).
Axes of the slice: x: 2, y: 2, z: 4, core: 2. Of those that a mesh axis runs over, the one named last changes fastest.
Arguments:
- amplitudes: bfloat16 [3, 160, 32, 5120], P(None, 'pair', 'row'), may hold values from -6 to 6
- integrals: bfloat16 [3, 5120, 5120], P(None, 'row', 'pair'), may hold values from -0.078125 to 0.078125
- occupied_irrep: int32 [32], replicated, may hold values from 0 to 7
- virtual_order: int32 [1280], replicated, may hold values from 0 to 1279, each once
- block_irreps: int32 [3], replicated, may hold values from 0 to 7
- occupied_energy: float32 [32], replicated, may hold values from -2 to -0.5
- virtual_energy: float32 [1280], replicated, may hold values from 1 to 4
Outputs:
- update: float32 [3, 160, 32, 5120], P(None, None, 'row', 'pair')
Inputs may be any that keep to these rules, and one draw needn't show every extreme that they name: virtual_order holds every virtual orbital once; entries g * 160 to g * 160 + 159 are the virtual orbitals of irrep g.
All inputs are finite; a program needn't handle non-finite values.
Results may differ from a plain program's by a relative error of at most 0.0003.
Values may be sent and summed in bfloat16 or wider, within the bound.
A program may use at most 128 MiB of HBM per device.

v0:
```python
import jax
import jax.numpy as jnp
from jax import lax
from jax.sharding import PartitionSpec as P

VIRG = 160


def shift_table(occupied_irrep, virtual_order, block_irreps, occupied_energy, virtual_energy):
    count_virt = virtual_energy.shape[0]
    orbital_ids = jnp.arange(count_virt, dtype=jnp.int32)
    matches = virtual_order[:, None] == orbital_ids[None, :]
    slot_energy = jnp.sum(jnp.where(matches, virtual_energy[None, :], jnp.float32(0.0)), axis=1)
    irrep_count = count_virt // VIRG
    energy_grid = slot_energy.reshape(irrep_count, VIRG)
    pair_irrep = jnp.bitwise_xor(block_irreps[:, None], occupied_irrep[None, :])
    irrep_ids = jnp.arange(irrep_count, dtype=jnp.int32)
    chosen = pair_irrep[:, None, None, :] == irrep_ids[None, :, None, None]
    picked = jnp.sum(jnp.where(chosen, energy_grid[None, :, :, None], jnp.float32(0.0)), axis=1)
    return picked - occupied_energy[None, None, :]


def body(
    amplitudes,
    integrals,
    occupied_irrep,
    virtual_order,
    block_irreps,
    occupied_energy,
    virtual_energy,
):
    block_count, virt_local, occ_local, pair_width = amplitudes.shape
    column_width = integrals.shape[2]
    shift = shift_table(
        occupied_irrep, virtual_order, block_irreps, occupied_energy, virtual_energy
    )
    occ_start = lax.axis_index("row") * occ_local
    col_start = lax.axis_index("pair") * column_width
    results = []
    for block in range(block_count):
        whole_rows = lax.all_gather(integrals[block], "row", axis=0, tiled=True)
        piece = lax.all_gather(amplitudes[block], "pair", axis=0, tiled=True)
        flat = piece.reshape(piece.shape[0] * piece.shape[1], piece.shape[2])
        product = jnp.dot(flat, whole_rows, preferred_element_type=jnp.float32)
        cycle_term = product.reshape(piece.shape[0], piece.shape[1], whole_rows.shape[1])
        row_shift = lax.dynamic_slice_in_dim(shift[block], occ_start, occ_local, 1)
        col_shift = lax.dynamic_slice_in_dim(
            shift[block].reshape(pair_width), col_start, column_width, 0
        )
        denominator = row_shift[:, :, None] + col_shift[None, None, :]
        results.append(cycle_term / denominator)
    return jnp.stack(results)


def solution(mesh):
    placed = (P(None, "pair", "row", None), P(None, "row", "pair"), P(), P(), P(), P(), P())
    return jax.shard_map(
        body, mesh=mesh, in_specs=placed, out_specs=P(None, None, "row", "pair"), check_vma=False
    )
```

profile of v0, /device:TPU:0, one launch (start us, length us, event | category | flops | bytes accessed | tf_op | source)
XLA Modules:
  0.0 626.3 jit_solution(1180767231952461776)
XLA Ops:
  6.5 0.0 all-gather.19.cloned.1.call-start
  6.5 4.8 fusion.21
  11.4 0.0 all-gather.19.cloned.1.call-update
  11.4 0.0 all-gather.17.cloned.1.call-start
  11.5 4.7 slice_bitcast_fusion.2
  16.2 0.0 copy-start.3
  16.2 0.0 all-gather.17.cloned.1.call-update
  16.2 0.0 all-gather.15.cloned.1.call-start
  16.3 0.7 all-gather.15.cloned.1.call-update
  17.0 0.0 all-gather.13.cloned.1.call-start
  17.0 0.5 all-gather.13.cloned.1.call-update
  17.5 0.0 all-gather.23.cloned.1.call-start
  17.6 0.5 all-gather.23.cloned.1.call-update
  18.1 0.0 all-gather.21.cloned.1.call-start
  18.2 0.5 all-gather.21.cloned.1.call-update
  18.7 0.0 copy-done.1
  18.7 0.0 copy-done.2
  18.7 1.0 select_reduce_fusion
  19.7 0.1 broadcast_in_dim.51
  19.8 0.0 copy-done.4
  19.8 0.0 copy-done.5
  19.8 0.1 broadcast_xor_fusion
  19.9 0.2 select_reduce_fusion.1
  20.0 0.0 copy-done.3
  20.0 0.1 broadcast_subtract_fusion
  20.1 0.1 copy.22
  20.2 0.1 reshape_squeeze.10
  20.3 0.1 copy.21
  20.4 0.1 copy.19
  20.6 0.1 reshape_squeeze.9
  20.6 0.1 dynamic_slice.21
  20.7 0.1 dynamic_slice.19
  20.8 0.1 copy.18
  20.9 0.1 copy.25
  21.0 0.1 reshape_squeeze.11
  21.1 0.1 dynamic_slice.23
  21.2 0.1 copy.24
  21.3 112.6 %all-gather.19.cloned.1.call-done = bf16[1,5120,640]{2,1,0:T(8,128)(2,1)} async-done(((bf16[1,1280,640]{2,1,0:T(8,128)(2,1)}), bf16[1,5120,640]{2,1,0:T(8,128)(2,1)}) %all-gather.19.cloned.1.call-update) | async-done | bytes 6553616 | tf_op jit(solution)/shard_map/all_gather | solution.py:41
  133.9 74.5 %all-gather.17.cloned.1.call-done = bf16[1,160,8,5120]{3,2,0,1:T(8,128)(2,1)} async-done(((bf16[1,20,8,5120]{3,2,0,1:T(8,128)(2,1)}), bf16[1,160,8,5120]{3,2,0,1:T(8,128)(2,1)}) %all-gather.17.cloned.1.call-update) | async-done | bytes 13107216 | tf_op jit(solution)/shard_map/all_gather | solution.py:42
  208.4 15.1 %divide_bitcast_fusion.1 = f32[1,160,8,640]{3,2,1,0:T(8,128)S(1)} fusion(bf16[1,5120,640]{2,1,0:T(8,128)(2,1)} %all-gather.19.cloned.1.call-done, bf16[1,160,8,5120]{3,2,0,1:T(8,128)(2,1)} %all-gather.17.cloned.1.call-done, f32[640]{0:T(1024)S(1)} %dynamic_slice.21, f32[160,8]{1,0:T(8,128)S(1)} %copy.21), kind=kOutput, calls=%fused_computation.13 | convolution fusion | flops 8390246400 | bytes 22945280 | tf_op jit(solution)/shard_map/dot_general | solution.py:44
  223.6 106.1 %all-gather.15.cloned.1.call-done = bf16[1,5120,640]{2,1,0:T(8,128)(2,1)} async-done(((bf16[1,1280,640]{2,1,0:T(8,128)(2,1)}), bf16[1,5120,640]{2,1,0:T(8,128)(2,1)}) %all-gather.15.cloned.1.call-update) | async-done | bytes 6553616 | tf_op jit(solution)/shard_map/all_gather | solution.py:41
  329.7 74.4 %all-gather.13.cloned.1.call-done = bf16[1,160,8,5120]{3,2,0,1:T(8,128)(2,1)} async-done(((bf16[1,20,8,5120]{3,2,0,1:T(8,128)(2,1)}), bf16[1,160,8,5120]{3,2,0,1:T(8,128)(2,1)}) %all-gather.13.cloned.1.call-update) | async-done | bytes 13107216 | tf_op jit(solution)/shard_map/all_gather | solution.py:42
  404.0 16.0 %divide_bitcast_fusion.2 = f32[1,160,8,640]{3,2,1,0:T(8,128)} fusion(bf16[1,5120,640]{2,1,0:T(8,128)(2,1)} %all-gather.15.cloned.1.call-done, bf16[1,160,8,5120]{3,2,0,1:T(8,128)(2,1)} %all-gather.13.cloned.1.call-done, f32[640]{0:T(1024)S(1)} %dynamic_slice.19, f32[160,8]{1,0:T(8,128)S(1)} %copy.18), kind=kOutput, calls=%fused_computation.14 | convolution fusion | flops 8390246400 | bytes 22945280 | tf_op jit(solution)/shard_map/dot_general | solution.py:44
  420.0 105.1 %all-gather.23.cloned.1.call-done = bf16[1,5120,640]{2,1,0:T(8,128)(2,1)} async-done(((bf16[1,1280,640]{2,1,0:T(8,128)(2,1)}), bf16[1,5120,640]{2,1,0:T(8,128)(2,1)}) %all-gather.23.cloned.1.call-update) | async-done | bytes 6553616 | tf_op jit(solution)/shard_map/all_gather | solution.py:41
  525.1 74.4 %all-gather.21.cloned.1.call-done = bf16[1,160,8,5120]{3,2,0,1:T(8,128)(2,1)} async-done(((bf16[1,20,8,5120]{3,2,0,1:T(8,128)(2,1)}), bf16[1,160,8,5120]{3,2,0,1:T(8,128)(2,1)}) %all-gather.21.cloned.1.call-update) | async-done | bytes 13107216 | tf_op jit(solution)/shard_map/all_gather | solution.py:42
  599.5 15.3 %divide_bitcast_fusion = f32[1,160,8,640]{3,2,1,0:T(8,128)S(1)} fusion(bf16[1,5120,640]{2,1,0:T(8,128)(2,1)} %all-gather.23.cloned.1.call-done, bf16[1,160,8,5120]{3,2,0,1:T(8,128)(2,1)} %all-gather.21.cloned.1.call-done, f32[640]{0:T(1024)S(1)} %dynamic_slice.23, f32[160,8]{1,0:T(8,128)S(1)} %copy.24), kind=kOutput, calls=%fused_computation.12 | convolution fusion | flops 8390246400 | bytes 22945280 | tf_op jit(solution)/shard_map/dot_general | solution.py:44
  614.8 0.0 copy-done
  614.8 4.7 pad_maximum_fusion
  (10 shorter events, 0.0 us)
Async XLA Ops:
  6.5 127.4 %all-gather.19.cloned.1.call-start = ((), (), s32[]{:S(2)}) async-start(), calls=%async_computation.3 | async-start | bytes 8192000 | tf_op jit(solution)/shard_map/all_gather | solution.py:41
  11.4 197.0 %all-gather.17.cloned.1.call-start = ((), (), s32[]{:S(2)}) async-start(), calls=%async_computation.2 | async-start | bytes 14745600 | tf_op jit(solution)/shard_map/all_gather | solution.py:42
  16.2 2.5 copy-start.1
  16.2 2.5 copy-start.2
  16.2 3.6 copy-start.4
  16.2 3.6 copy-start.5
  16.2 3.9 copy-start.3
  16.2 313.4 %all-gather.15.cloned.1.call-start = ((), (), s32[]{:S(2)}) async-start(), calls=%async_computation.1 | async-start | bytes 8192000 | tf_op jit(solution)/shard_map/all_gather | solution.py:41
  17.0 387.1 %all-gather.13.cloned.1.call-start = ((), (), s32[]{:S(2)}) async-start(), calls=%async_computation | async-start | bytes 14745600 | tf_op jit(solution)/shard_map/all_gather | solution.py:42
  17.5 507.6 %all-gather.23.cloned.1.call-start = ((), (), s32[]{:S(2)}) async-start(), calls=%async_computation.5 | async-start | bytes 8192000 | tf_op jit(solution)/shard_map/all_gather | solution.py:41
  18.1 581.3 %all-gather.21.cloned.1.call-start = ((), (), s32[]{:S(2)}) async-start(), calls=%async_computation.4 | async-start | bytes 14745600 | tf_op jit(solution)/shard_map/all_gather | solution.py:42
  599.5 15.3 %copy-start = (f32[1,160,8,640]{3,2,1,0:T(8,128)S(1)}, f32[1,160,8,640]{3,2,1,0:T(8,128)}, u32[]{:S(2)}) copy-start(f32[1,160,8,640]{3,2,1,0:T(8,128)} %divide_bitcast_fusion.2) | copy-start | bytes 9830404
Sparse Core Ops, SparseCore 0:
  11.5 122.3 all-gather.18
  135.8 72.5 all-gather.16
  210.0 119.6 all-gather.14
  331.4 72.5 all-gather.12
  405.4 119.6 all-gather.22
  526.9 72.5 all-gather.20
where the time goes:
time: 626 us
  waiting for transfers between devices  549 us (88%)
  matrix products  46.4 us (7%)
  between operations  13.6 us (2%)
  local copies, waits for them, and re-layouts  10.8 us (2%)
    all_gather x3, waiting for transfers between devices, body(): whole_rows = lax.all_gather(integrals[block], 'row', axis=0, tiled=True)  324 us
    all_gather x3, waiting for transfers between devices, body(): piece = lax.all_gather(amplitudes[block], 'pair', axis=0, tiled=True)  223 us
    dot_general x3, matrix products, body(): product = jnp.dot(flat, whole_rows, preferred_element_type=jnp.float32)  46.4 us
  transfers between devices with their start and end apart: 6, of which 6 were waited for; matrix products, arithmetic and copies ran while one was open for 6% of the time, Pallas kernels for 0%

commit v1 on v0

--- a/solution.py
+++ b/solution.py
@@ -52,8 +52,89 @@
     return jnp.stack(results)
 
 
+def gather_integrals(mine):
+    row = lax.axis_index("row")
+    near = lax.ppermute(mine, "row", [(0, 1), (1, 0), (2, 3), (3, 2)])
+    far_inner = lax.ppermute(mine, "row", [(1, 2), (2, 1)])
+    far_outer = lax.ppermute(near, "row", [(1, 2), (2, 1)])
+    end_inner = lax.ppermute(far_inner, "row", [(1, 0), (2, 3)])
+    end_outer = lax.ppermute(far_outer, "row", [(1, 0), (2, 3)])
+    inner = jnp.where((row == 1) | (row == 2), far_inner, end_inner)
+    outer = jnp.where((row == 1) | (row == 2), far_outer, end_outer)
+    even = row % 2 == 0
+    first = jnp.where(even, mine, near)
+    second = jnp.where(even, near, mine)
+    low = row < 2
+    return jnp.concatenate(
+        [
+            jnp.where(low, first, outer),
+            jnp.where(low, second, inner),
+            jnp.where(low, inner, first),
+            jnp.where(low, outer, second),
+        ]
+    )
+
+
+def gather_amplitudes(mine):
+    pair = lax.axis_index("pair")
+    spot = pair // 2
+    whole = jnp.zeros((4,) + mine.shape, mine.dtype)
+    whole = lax.dynamic_update_slice_in_dim(whole, mine[None], spot, 0)
+    for step in (1, 2, 3):
+        came = lax.ppermute(mine, "pair", [(p, p ^ (2 * step)) for p in range(8)])
+        whole = lax.dynamic_update_slice_in_dim(whole, came[None], spot ^ step, 0)
+    other = lax.ppermute(whole, "pair", [(p, p ^ 1) for p in range(8)])
+    return whole, other
+
+
+def linked_body(
+    amplitudes,
+    integrals,
+    occupied_irrep,
+    virtual_order,
+    block_irreps,
+    occupied_energy,
+    virtual_energy,
+):
+    block_count, virt_local, occ_local, pair_width = amplitudes.shape
+    column_width = integrals.shape[2]
+    shift = shift_table(
+        occupied_irrep, virtual_order, block_irreps, occupied_energy, virtual_energy
+    )
+    occ_start = lax.axis_index("row") * occ_local
+    pair = lax.axis_index("pair")
+    core = pair % 2
+    results = []
+    for block in range(block_count):
+        whole_rows = gather_integrals(integrals[block])
+        pieces = gather_amplitudes(amplitudes[block])
+        row_shift = lax.dynamic_slice_in_dim(shift[block], occ_start, occ_local, 1)
+        row_shift = row_shift.reshape(4, 2, virt_local, occ_local)
+        col_shift = lax.dynamic_slice_in_dim(
+            shift[block].reshape(pair_width), pair * column_width, column_width, 0
+        )
+        halves = []
+        for side, piece in enumerate(pieces):
+            product = jnp.dot(
+                piece.reshape(-1, pair_width), whole_rows, preferred_element_type=jnp.float32
+            ).reshape(4, virt_local, occ_local, column_width)
+            part_shift = lax.dynamic_index_in_dim(row_shift, core ^ side, 1, keepdims=False)
+            halves.append(product / (part_shift[..., None] + col_shift))
+        even = core == 0
+        both = jnp.stack(
+            [jnp.where(even, halves[0], halves[1]), jnp.where(even, halves[1], halves[0])], 1
+        )
+        results.append(both.reshape(8 * virt_local, occ_local, column_width))
+    return jnp.stack(results)
+
+
 def solution(mesh):
     placed = (P(None, "pair", "row", None), P(None, "row", "pair"), P(), P(), P(), P(), P())
+    linked = mesh.shape["pair"] == 8 and mesh.shape["row"] == 4
     return jax.shard_map(
-        body, mesh=mesh, in_specs=placed, out_specs=P(None, None, "row", "pair"), check_vma=False
+        linked_body if linked else body,
+        mesh=mesh,
+        in_specs=placed,
+        out_specs=P(None, None, "row", "pair"),
+        check_vma=False,
     )

time: 626 us -> 565 us (0.903); the launches traced: 626 us -> 556 us
  waiting for transfers between devices: 549 us -> 387 us
  local copies, waits for them, and re-layouts: 10.8 us -> 51 us
  starting transfers between devices: 0.2 us -> 30.4 us
  matrix products: 46.4 us -> 64.9 us
  other arithmetic: 6 us -> 22.2 us
  between operations: 13.6 us -> 0.72 us
    all_gather x6 -> x0, waiting for transfers between devices: 547 us -> none  [the longest x3 324 us: body(): whole_rows = lax.all_gather(integrals[block], 'row', axis=0, tiled=True)]
    ppermute x0 -> x27, waiting for transfers between devices: none -> 387 us  [the longest x9 195 us: gather_amplitudes(): came = lax.ppermute(mine, 'pair', [(p, p ^ 2 * step) for p in range(8)])]
    ppermute x0 -> x27, starting transfers between devices: none -> 30.4 us  [the longest x9 12.7 us: gather_amplitudes(): came = lax.ppermute(mine, 'pair', [(p, p ^ 2 * step) for p in range(8)])]
    dynamic_update_slice x0 -> x11, local copies, waits for them, and re-layouts: none -> 22.8 us  [the longest x9 17.4 us: gather_amplitudes(): whole = lax.dynamic_update_slice_in_dim(whole, came[None], spot ^ step, 0)]
    dot_general x3 -> x6, matrix products: 46.4 us -> 64.9 us  [linked_body(): jnp.dot(piece.reshape(-1, pair_width), whole_rows, preferred_element_type...]
    select_n x0 -> x3, other arithmetic: none -> 9.99 us  [gather_integrals(): jnp.where(low, first, outer)]
    another operation x3 -> x9, local copies, waits for them, and re-layouts: 0.25 us -> 9.36 us  [body(): shift[block].reshape(pair_width)]
    squeeze x0 -> x2, local copies, waits for them, and re-layouts: none -> 7.41 us  [the longest x1 5.26 us: linked_body(): pieces = gather_amplitudes(amplitudes[block])]
  transfers between devices with their start and end apart: 6 -> 27, of which waited for: 6 -> 10; matrix products, arithmetic and copies ran while one was open for 6% -> 18% of each run, Pallas kernels for 0% -> 0%
where the time goes in v1:
time: 565 us; the launch traced here: 556 us
  waiting for transfers between devices  387 us (68%)
  matrix products  64.9 us (11%)
  local copies, waits for them, and re-layouts  51 us (9%)
  starting transfers between devices  30.4 us (5%)
  other arithmetic  22.2 us (4%)
    ppermute x9, waiting for transfers between devices, gather_amplitudes(): came = lax.ppermute(mine, 'pair', [(p, p ^ 2 * step) for p in range(8)])  195 us
    ppermute x3, waiting for transfers between devices, gather_integrals(): end_outer = lax.ppermute(far_outer, 'row', [(1, 0), (2, 3)])  96.6 us
    ppermute x3, waiting for transfers between devices, gather_integrals(): end_inner = lax.ppermute(far_inner, 'row', [(1, 0), (2, 3)])  95.8 us
    dot_general x6, matrix products, linked_body(): jnp.dot(piece.reshape(-1, pair_width), whole_rows, preferred_element_type...  64.9 us
    dynamic_update_slice x9, local copies, waits for them, and re-layouts, gather_amplitudes(): whole = lax.dynamic_update_slice_in_dim(whole, came[None], spot ^ step, 0)  17.4 us
    ppermute x9, starting transfers between devices, gather_amplitudes(): came = lax.ppermute(mine, 'pair', [(p, p ^ 2 * step) for p in range(8)])  12.7 us
  transfers between devices with their start and end apart: 27, of which 10 were waited for; matrix products, arithmetic and copies ran while one was open for 18% of the time, Pallas kernels for 0%

profile of v1, /device:TPU:0, one launch (start us, length us, event | category | flops | bytes accessed | tf_op | source)
XLA Modules:
  0.0 556.2 jit_solution(1807885105584102933)
XLA Ops:
  0.8 5.3 slice_bitcast_fusion.5
  6.1 3.0 collective-permute-start
  9.1 1.5 collective-permute-start.1
  10.7 2.1 slice_bitcast_fusion.2
  12.8 2.0 collective-permute-start.3
  14.9 1.5 collective-permute-start.9
  18.0 3.5 broadcast.35.clone.2
  21.5 2.7 slice_dynamic-update-slice_fusion.1
  24.2 3.6 broadcast.35.clone
  27.8 2.7 slice_dynamic-update-slice_fusion
  39.1 7.0 %collective-permute-done = bf16[20,8,5120]{2,1,0:T(8,128)(2,1)} collective-permute-done((bf16[20,8,5120]{2,1,0:T(8,128)(2,1)}, bf16[20,8,5120]{2,1,0:T(8,128)(2,1)}, u32[]{:S(2)}, u32[]{:S(2)}) %collective-permute-start) | collective-permute-done | bytes 1638432 | tf_op jit(solution)/shard_map/ppermute | solution.py:84
  46.8 2.7 bitcast_dynamic-update-slice_fusion.8
  49.5 66.0 %collective-permute-done.9 = bf16[20,8,5120]{2,1,0:T(8,128)(2,1)} collective-permute-done((bf16[20,8,5120]{2,1,0:T(8,128)(2,1)}, bf16[20,8,5120]{2,1,0:T(8,128)(2,1)}, u32[]{:S(2)}, u32[]{:S(2)}) %collective-permute-start.9) | collective-permute-done | bytes 1638432 | tf_op jit(solution)/shard_map/ppermute | solution.py:84
  115.5 1.8 collective-permute-start.10
  117.3 2.8 bitcast_dynamic-update-slice_fusion.5
  120.0 1.4 collective-permute-start.11
  121.4 1.6 collective-permute-start.12
  123.0 2.7 bitcast_dynamic-update-slice_fusion.7
  127.2 60.7 %collective-permute-done.10 = bf16[20,8,5120]{2,1,0:T(8,128)(2,1)S(1)} collective-permute-done((bf16[20,8,5120]{2,1,0:T(8,128)(2,1)}, bf16[20,8,5120]{2,1,0:T(8,128)(2,1)S(1)}, u32[]{:S(2)}, u32[]{:S(2)}) %collective-permute-start.10) | collective-permute-done | bytes 1638432 | tf_op jit(solution)/shard_map/ppermute | solution.py:84
  187.8 1.4 collective-permute-start.19
  190.5 1.5 collective-permute-start.20
  192.0 1.6 collective-permute-start.21
  193.6 2.9 bitcast_dynamic-update-slice_fusion.6
  198.1 60.9 %collective-permute-done.19 = bf16[20,8,5120]{2,1,0:T(8,128)(2,1)S(1)} collective-permute-done((bf16[20,8,5120]{2,1,0:T(8,128)(2,1)S(1)}, bf16[20,8,5120]{2,1,0:T(8,128)(2,1)S(1)}, u32[]{:S(2)}, u32[]{:S(2)}) %collective-permute-start.19) | collective-permute-done | bytes 1638432 | tf_op jit(solution)/shard_map/ppermute | solution.py:84
  259.0 1.3 collective-permute-start.7
  263.8 1.3 collective-permute-start.16
  265.8 33.8 %collective-permute-done.7 = bf16[1280,640]{1,0:T(8,128)(2,1)S(1)} collective-permute-done((bf16[1280,640]{1,0:T(8,128)(2,1)S(1)}, bf16[1280,640]{1,0:T(8,128)(2,1)S(1)}, u32[]{:S(2)}, u32[]{:S(2)}) %collective-permute-start.7) | collective-permute-done | bytes 1638432 | tf_op jit(solution)/shard_map/ppermute | solution.py:60
  302.2 1.3 collective-permute-start.14
  304.7 30.0 %collective-permute-done.16 = bf16[1280,640]{1,0:T(8,128)(2,1)S(1)} collective-permute-done((bf16[1280,640]{1,0:T(8,128)(2,1)S(1)}, bf16[1280,640]{1,0:T(8,128)(2,1)S(1)}, u32[]{:S(2)}, u32[]{:S(2)}) %collective-permute-start.16) | collective-permute-done | bytes 1638432 | tf_op jit(solution)/shard_map/ppermute | solution.py:60
  334.7 1.3 collective-permute-start.25
  336.0 33.8 %collective-permute-done.5 = bf16[1280,640]{1,0:T(8,128)(2,1)S(1)} collective-permute-done((bf16[1280,640]{1,0:T(8,128)(2,1)S(1)}, bf16[1280,640]{1,0:T(8,128)(2,1)S(1)}, u32[]{:S(2)}, u32[]{:S(2)}) %collective-permute-start.5) | collective-permute-done | bytes 1638432 | tf_op jit(solution)/shard_map/ppermute | solution.py:61
  369.8 1.3 collective-permute-start.23
  371.1 2.6 broadcast_select_fusion.23
  373.8 31.2 %collective-permute-done.14 = bf16[1280,640]{1,0:T(8,128)(2,1)S(1)} collective-permute-done((bf16[1280,640]{1,0:T(8,128)(2,1)S(1)}, bf16[1280,640]{1,0:T(8,128)(2,1)S(1)}, u32[]{:S(2)}, u32[]{:S(2)}) %collective-permute-start.14) | collective-permute-done | bytes 1638432 | tf_op jit(solution)/shard_map/ppermute | solution.py:61
  404.9 3.1 broadcast_select_fusion.19
  408.0 32.0 %collective-permute-done.25 = bf16[1280,640]{1,0:T(8,128)(2,1)S(1)} collective-permute-done((bf16[1280,640]{1,0:T(8,128)(2,1)S(1)}, bf16[1280,640]{1,0:T(8,128)(2,1)S(1)}, u32[]{:S(2)}, u32[]{:S(2)}) %collective-permute-start.25) | collective-permute-done | bytes 1638432 | tf_op jit(solution)/shard_map/ppermute | solution.py:60
  440.0 31.6 %collective-permute-done.23 = bf16[1280,640]{1,0:T(8,128)(2,1)} collective-permute-done((bf16[1280,640]{1,0:T(8,128)(2,1)S(1)}, bf16[1280,640]{1,0:T(8,128)(2,1)}, u32[]{:S(2)}, u32[]{:S(2)}) %collective-permute-start.23) | collective-permute-done | bytes 1638432 | tf_op jit(solution)/shard_map/ppermute | solution.py:61
  471.7 4.3 broadcast_select_fusion.15
  476.0 10.8 %add_divide_fusion.4 = f32[4,20,8,640]{3,2,1,0:T(8,128)} fusion(bf16[4,20,8,5120]{3,2,1,0:T(8,128)(2,1)} %collective-permute-done.8, bf16[1280,640]{1,0:T(8,128)(2,1)} %get-tuple-element.6, bf16[1280,640]{1,0:T(8,128)(2,1)} %get-tuple-element.17, bf16[1280,640]{1,0:T(8,128)(2,1)} %get-tuple-element.18, bf16[1280,640]{1,0:T(8,128)(2,1)S(1)} %get-tuple-element.5, ...), kind=kOutput, calls=%fused_computation.36 | convolution fusion | flops 4221337600 | bytes 14750720 | tf_op jit(solution)/shard_map/dot_general | solution.py:118
  486.8 10.4 %select_bitcast_fusion.5 = (f32[4,1,20,8,640]{4,3,2,0,1:T(8,128)}, f32[4,1,20,8,640]{4,3,2,0,1:T(8,128)}) fusion(f32[4,20,8,640]{3,2,1,0:T(8,128)} %add_divide_fusion.4, pred[]{:T(512)S(6)} %eq.30, f32[640]{0:T(1024)S(1)} %dynamic_slice.39, f32[4,20,8]{2,1,0:T(8,128)} %copy.33, bf16[4,20,8,5120]{3,2,1,0:T(8,128)(2,1)S(1)} %bitcast.131, ...), kind=kOutput, calls=%fused_computation.35 | convolution fusion | flops 4222156800 | bytes 18027520 | tf_op jit(solution)/shard_map/dot_general | solution.py:118
  497.2 2.2 pad_maximum_fusion.1
  501.8 10.0 %add_divide_fusion.2 = f32[4,20,8,640]{3,2,1,0:T(8,128)} fusion(bf16[4,20,8,5120]{3,2,1,0:T(8,128)(2,1)} %collective-permute-done.17, bf16[1280,640]{1,0:T(8,128)(2,1)S(1)} %copy-done.4, bf16[1280,640]{1,0:T(8,128)(2,1)S(1)} %copy-done.5, bf16[1280,640]{1,0:T(8,128)(2,1)} %get-tuple-element.20, bf16[1280,640]{1,0:T(8,128)(2,1)S(1)} %copy-done.3, ...), kind=kOutput, calls=%fused_computation.31 | convolution fusion | flops 4221337600 | bytes 14750720 | tf_op jit(solution)/shard_map/dot_general | solution.py:118
  511.8 11.4 %select_bitcast_fusion.3 = (f32[4,1,20,8,640]{4,3,2,0,1:T(8,128)}, f32[4,1,20,8,640]{4,3,2,0,1:T(8,128)}) fusion(f32[4,20,8,640]{3,2,1,0:T(8,128)} %add_divide_fusion.2, pred[]{:T(512)S(6)} %eq.30, f32[640]{0:T(1024)S(1)} %copy-done.14, f32[4,20,8]{2,1,0:T(8,128)S(1)} %copy-done.10, bf16[4,20,8,5120]{3,2,1,0:T(8,128)(2,1)} %bitcast_dynamic-update-slice_fusion.3, ...), kind=kOutput, calls=%fused_computation.30 | convolution fusion | flops 4222156800 | bytes 18027520 | tf_op jit(solution)/shard_map/dot_general | solution.py:118
  523.1 2.2 pad_maximum_fusion.2
  526.7 10.6 %add_divide_fusion = f32[4,20,8,640]{3,2,1,0:T(8,128)} fusion(bf16[4,20,8,5120]{3,2,1,0:T(8,128)(2,1)} %collective-permute-done.26, bf16[1280,640]{1,0:T(8,128)(2,1)S(1)} %copy-done.2, bf16[1280,640]{1,0:T(8,128)(2,1)} %get-tuple-element.21, bf16[1280,640]{1,0:T(8,128)(2,1)} %get-tuple-element.22, bf16[1280,640]{1,0:T(8,128)(2,1)S(1)} %get-tuple-element.13, ...), kind=kOutput, calls=%fused_computation.26 | convolution fusion | flops 4221337600 | bytes 14750720 | tf_op jit(solution)/shard_map/dot_general | solution.py:118
  537.4 11.7 %select_bitcast_fusion.1 = (f32[4,1,20,8,640]{4,3,2,0,1:T(8,128)}, f32[4,1,20,8,640]{4,3,2,0,1:T(8,128)}) fusion(f32[4,20,8,640]{3,2,1,0:T(8,128)} %add_divide_fusion, pred[]{:T(512)S(6)} %eq.30, f32[640]{0:T(1024)S(1)} %copy-done.13, f32[4,20,8]{2,1,0:T(8,128)S(1)} %copy-done.9, bf16[4,20,8,5120]{3,2,1,0:T(8,128)(2,1)} %bitcast_dynamic-update-slice_fusion, ...), kind=kOutput, calls=%fused_computation.25 | convolution fusion | flops 4222156800 | bytes 18027520 | tf_op jit(solution)/shard_map/dot_general | solution.py:118
  549.1 2.2 pad_maximum_fusion.3
  551.5 4.5 pad_maximum_fusion
  (119 shorter events, 28.0 us)
Async XLA Ops:
  0.0 10.7 %slice-start = ((s8[4915200]{0:T(1024)(128)(4,1)}), s8[4194304]{0:T(1024)(128)(4,1)S(1)}, s32[]{:S(2)}) async-start(s8[4915200]{0:T(1024)(128)(4,1)} %bitcast.123), calls=%async_computation | async-start | bytes 8388608
  0.8 9.9 %slice-start.1 = ((s8[4915200]{0:T(1024)(128)(4,1)}), s8[720896]{0:T(1024)(128)(4,1)S(1)}, s32[]{:S(2)}) async-start(s8[4915200]{0:T(1024)(128)(4,1)} %bitcast.123), calls=%async_computation.1 | async-start | bytes 1441792
  6.1 6.7 %copy-start = (bf16[4,20,8,5120]{3,2,1,0:T(8,128)(2,1)}, bf16[4,20,8,5120]{3,2,1,0:T(8,128)(2,1)S(1)}, u32[]{:S(2)}) copy-start(bf16[4,20,8,5120]{3,2,1,0:T(8,128)(2,1)S(1)} %get-tuple-element.29) | copy-start | bytes 19660804
  6.1 10.3 %copy-start.11 = (f32[1280]{0:T(1024)S(1)}, f32[1280]{0:T(1024)}, u32[]{:S(2)}) copy-start(f32[1280]{0:T(1024)} %param.13) | copy-start | bytes 15364
  6.1 10.3 %copy-start.12 = (s32[1280]{0:T(1024)S(1)}, s32[1280]{0:T(1024)}, u32[]{:S(2)}) copy-start(s32[1280]{0:T(1024)} %param.10) | copy-start | bytes 15364
  6.1 11.3 %copy-start.16 = (s32[32]{0:T(128)S(1)}, s32[32]{0:T(128)}, u32[]{:S(2)}) copy-start(s32[32]{0:T(128)} %param.9) | copy-start | bytes 388
  6.1 11.3 %copy-start.17 = (s32[3]{0:T(128)S(1)}, s32[3]{0:T(128)}, u32[]{:S(2)}) copy-start(s32[3]{0:T(128)} %param.11) | copy-start | bytes 40
  6.1 11.6 %copy-start.15 = (f32[32]{0:T(128)S(1)}, f32[32]{0:T(128)}, u32[]{:S(2)}) copy-start(f32[32]{0:T(128)} %param.12) | copy-start | bytes 388
  6.1 39.9 %collective-permute-start = (bf16[20,8,5120]{2,1,0:T(8,128)(2,1)}, bf16[20,8,5120]{2,1,0:T(8,128)(2,1)}, u32[]{:S(2)}, u32[]{:S(2)}) collective-permute-start(bf16[20,8,5120]{2,1,0:T(8,128)(2,1)} %get-tuple-element.26), channel_id=1, source_target_pairs={{0,8},{4,12},{8,0},{12,4},{16,24},{20,28},{24,16},{28,20},{1,9},{5... | collective-permute-start | bytes 4915208 | tf_op jit(solution)/shard_map/ppermute | solution.py:84
  9.1 110.9 %collective-permute-start.1 = (bf16[20,8,5120]{2,1,0:T(8,128)(2,1)}, bf16[20,8,5120]{2,1,0:T(8,128)(2,1)}, u32[]{:S(2)}, u32[]{:S(2)}) collective-permute-start(bf16[20,8,5120]{2,1,0:T(8,128)(2,1)} %get-tuple-element.26), channel_id=1, source_target_pairs={{0,16},{4,20},{8,24},{12,28},{16,0},{20,4},{24,8},{28,12},{1,17},{... | collective-permute-start | bytes 4915208 | tf_op jit(solution)/shard_map/ppermute | solution.py:84
  10.6 110.8 %collective-permute-start.2 = (bf16[20,8,5120]{2,1,0:T(8,128)(2,1)}, bf16[20,8,5120]{2,1,0:T(8,128)(2,1)}, u32[]{:S(2)}, u32[]{:S(2)}) collective-permute-start(bf16[20,8,5120]{2,1,0:T(8,128)(2,1)} %get-tuple-element.26), channel_id=1, source_target_pairs={{0,24},{4,28},{8,16},{12,20},{16,8},{20,12},{24,0},{28,4},{1,25},{... | collective-permute-start | bytes 4915208 | tf_op jit(solution)/shard_map/ppermute | solution.py:84
  12.8 113.0 %collective-permute-start.3 = (bf16[1280,640]{1,0:T(8,128)(2,1)}, bf16[1280,640]{1,0:T(8,128)(2,1)S(1)}, u32[]{:S(2)}, u32[]{:S(2)}) collective-permute-start(bf16[1280,640]{1,0:T(8,128)(2,1)} %get-tuple-element.23), channel_id=1, source_target_pairs={{0,1},{1,0},{2,3},{3,2},{4,5},{5,4},{6,7},{7,6},{8,9},{9,8},{10,11... | collective-permute-start | bytes 4915208 | tf_op jit(solution)/shard_map/ppermute | solution.py:57
  14.9 100.6 %collective-permute-start.9 = (bf16[20,8,5120]{2,1,0:T(8,128)(2,1)}, bf16[20,8,5120]{2,1,0:T(8,128)(2,1)}, u32[]{:S(2)}, u32[]{:S(2)}) collective-permute-start(bf16[20,8,5120]{2,1,0:T(8,128)(2,1)} %get-tuple-element.27), channel_id=1, source_target_pairs={{0,8},{4,12},{8,0},{12,4},{16,24},{20,28},{24,16},{28,20},{1,9},{5... | collective-permute-start | bytes 4915208 | tf_op jit(solution)/shard_map/ppermute | solution.py:84
  46.1 80.5 %collective-permute-start.6 = (bf16[1280,640]{1,0:T(8,128)(2,1)}, bf16[1280,640]{1,0:T(8,128)(2,1)S(1)}, u32[]{:S(2)}, u32[]{:S(2)}) collective-permute-start(bf16[1280,640]{1,0:T(8,128)(2,1)} %get-tuple-element.23), channel_id=1, source_target_pairs={{1,2},{2,1},{5,6},{6,5},{9,10},{10,9},{13,14},{14,13},{17,18},{18,... | collective-permute-start | bytes 4915208 | tf_op jit(solution)/shard_map/ppermute | solution.py:58
  49.5 71.9 %copy-start.1 = (bf16[1280,640]{1,0:T(8,128)(2,1)S(1)}, bf16[1280,640]{1,0:T(8,128)(2,1)}, u32[]{:S(2)}) copy-start(bf16[1280,640]{1,0:T(8,128)(2,1)} %get-tuple-element.25) | copy-start | bytes 4915204
  115.5 72.3 %collective-permute-start.10 = (bf16[20,8,5120]{2,1,0:T(8,128)(2,1)}, bf16[20,8,5120]{2,1,0:T(8,128)(2,1)S(1)}, u32[]{:S(2)}, u32[]{:S(2)}) collective-permute-start(bf16[20,8,5120]{2,1,0:T(8,128)(2,1)} %get-tuple-element.27), channel_id=1, source_target_pairs={{0,16},{4,20},{8,24},{12,28},{16,0},{20,4},{24,8},{28,12},{1,17},{... | collective-permute-start | bytes 4915208 | tf_op jit(solution)/shard_map/ppermute | solution.py:84
  120.0 70.5 %collective-permute-start.11 = (bf16[20,8,5120]{2,1,0:T(8,128)(2,1)}, bf16[20,8,5120]{2,1,0:T(8,128)(2,1)S(1)}, u32[]{:S(2)}, u32[]{:S(2)}) collective-permute-start(bf16[20,8,5120]{2,1,0:T(8,128)(2,1)} %get-tuple-element.27), channel_id=1, source_target_pairs={{0,24},{4,28},{8,16},{12,20},{16,8},{20,12},{24,0},{28,4},{1,25},{... | collective-permute-start | bytes 4915208 | tf_op jit(solution)/shard_map/ppermute | solution.py:84
  121.4 5.1 copy-start.7
  121.4 70.6 %collective-permute-start.12 = (bf16[1280,640]{1,0:T(8,128)(2,1)S(1)}, bf16[1280,640]{1,0:T(8,128)(2,1)S(1)}, u32[]{:S(2)}, u32[]{:S(2)}) collective-permute-start(bf16[1280,640]{1,0:T(8,128)(2,1)S(1)} %copy-done.1), channel_id=1, source_target_pairs={{0,1},{1,0},{2,3},{3,2},{4,5},{5,4},{6,7},{7,6},{8,9},{9,8},{10,11... | collective-permute-start | bytes 4915208 | tf_op jit(solution)/shard_map/ppermute | solution.py:57
  125.8 70.7 %collective-permute-start.15 = (bf16[1280,640]{1,0:T(8,128)(2,1)S(1)}, bf16[1280,640]{1,0:T(8,128)(2,1)S(1)}, u32[]{:S(2)}, u32[]{:S(2)}) collective-permute-start(bf16[1280,640]{1,0:T(8,128)(2,1)S(1)} %copy-done.1), channel_id=1, source_target_pairs={{1,2},{2,1},{5,6},{6,5},{9,10},{10,9},{13,14},{14,13},{17,18},{18,... | collective-permute-start | bytes 4915208 | tf_op jit(solution)/shard_map/ppermute | solution.py:58
  126.6 70.7 %collective-permute-start.18 = (bf16[20,8,5120]{2,1,0:T(8,128)(2,1)S(1)}, bf16[20,8,5120]{2,1,0:T(8,128)(2,1)S(1)}, u32[]{:S(2)}, u32[]{:S(2)}) collective-permute-start(bf16[20,8,5120]{2,1,0:T(8,128)(2,1)S(1)} %copy-done.7), channel_id=1, source_target_pairs={{0,8},{4,12},{8,0},{12,4},{16,24},{20,28},{24,16},{28,20},{1,9},{5... | collective-permute-start | bytes 4915208 | tf_op jit(solution)/shard_map/ppermute | solution.py:84
  187.8 71.2 %collective-permute-start.19 = (bf16[20,8,5120]{2,1,0:T(8,128)(2,1)S(1)}, bf16[20,8,5120]{2,1,0:T(8,128)(2,1)S(1)}, u32[]{:S(2)}, u32[]{:S(2)}) collective-permute-start(bf16[20,8,5120]{2,1,0:T(8,128)(2,1)S(1)} %copy-done.7), channel_id=1, source_target_pairs={{0,16},{4,20},{8,24},{12,28},{16,0},{20,4},{24,8},{28,12},{1,17},{... | collective-permute-start | bytes 4915208 | tf_op jit(solution)/shard_map/ppermute | solution.py:84
  190.5 71.0 %collective-permute-start.20 = (bf16[20,8,5120]{2,1,0:T(8,128)(2,1)S(1)}, bf16[20,8,5120]{2,1,0:T(8,128)(2,1)S(1)}, u32[]{:S(2)}, u32[]{:S(2)}) collective-permute-start(bf16[20,8,5120]{2,1,0:T(8,128)(2,1)S(1)} %copy-done.7), channel_id=1, source_target_pairs={{0,24},{4,28},{8,16},{12,20},{16,8},{20,12},{24,0},{28,4},{1,25},{... | collective-permute-start | bytes 4915208 | tf_op jit(solution)/shard_map/ppermute | solution.py:84
  192.0 69.5 %collective-permute-start.21 = (bf16[1280,640]{1,0:T(8,128)(2,1)S(1)}, bf16[1280,640]{1,0:T(8,128)(2,1)S(1)}, u32[]{:S(2)}, u32[]{:S(2)}) collective-permute-start(bf16[1280,640]{1,0:T(8,128)(2,1)S(1)} %get-tuple-element.24), channel_id=1, source_target_pairs={{0,1},{1,0},{2,3},{3,2},{4,5},{5,4},{6,7},{7,6},{8,9},{9,8},{10,11... | collective-permute-start | bytes 4915208 | tf_op jit(solution)/shard_map/ppermute | solution.py:57
  193.6 177.5 %slice-start.2 = ((s8[4915200]{0:T(1024)(128)(4,1)}), s8[4194304]{0:T(1024)(128)(4,1)S(1)}, s32[]{:S(2)}) async-start(s8[4915200]{0:T(1024)(128)(4,1)} %bitcast.125), calls=%async_computation.2 | async-start | bytes 8388608
  196.5 67.2 %collective-permute-start.24 = (bf16[1280,640]{1,0:T(8,128)(2,1)S(1)}, bf16[1280,640]{1,0:T(8,128)(2,1)S(1)}, u32[]{:S(2)}, u32[]{:S(2)}) collective-permute-start(bf16[1280,640]{1,0:T(8,128)(2,1)S(1)} %get-tuple-element.24), channel_id=1, source_target_pairs={{1,2},{2,1},{5,6},{6,5},{9,10},{10,9},{13,14},{14,13},{17,18},{18,... | collective-permute-start | bytes 4915208 | tf_op jit(solution)/shard_map/ppermute | solution.py:58
  197.3 67.8 %collective-permute-start.4 = (bf16[1280,640]{1,0:T(8,128)(2,1)S(1)}, bf16[1280,640]{1,0:T(8,128)(2,1)S(1)}, u32[]{:S(2)}, u32[]{:S(2)}) collective-permute-start(bf16[1280,640]{1,0:T(8,128)(2,1)S(1)} %collective-permute-done.3), channel_id=1, source_target_pairs={{1,2},{2,1},{5,6},{6,5},{9,10},{10,9},{13,14},{14,13},{17,18},{18,... | collective-permute-start | bytes 4915208 | tf_op jit(solution)/shard_map/ppermute | solution.py:59
  259.0 40.6 %collective-permute-start.7 = (bf16[1280,640]{1,0:T(8,128)(2,1)S(1)}, bf16[1280,640]{1,0:T(8,128)(2,1)S(1)}, u32[]{:S(2)}, u32[]{:S(2)}) collective-permute-start(bf16[1280,640]{1,0:T(8,128)(2,1)S(1)} %collective-permute-done.6), channel_id=1, source_target_pairs={{1,0},{2,3},{5,4},{6,7},{9,8},{10,11},{13,12},{14,15},{17,16},{18,... | collective-permute-start | bytes 4915208 | tf_op jit(solution)/shard_map/ppermute | solution.py:60
  261.5 109.6 %slice-start.3 = ((s8[4915200]{0:T(1024)(128)(4,1)}), s8[720896]{0:T(1024)(128)(4,1)S(1)}, s32[]{:S(2)}) async-start(s8[4915200]{0:T(1024)(128)(4,1)} %bitcast.125), calls=%async_computation.3 | async-start | bytes 1441792
  261.5 214.4 %collective-permute-start.8 = (bf16[4,20,8,5120]{3,2,1,0:T(8,128)(2,1)}, bf16[4,20,8,5120]{3,2,1,0:T(8,128)(2,1)}, u32[]{:S(2)}, u32[]{:S(2)}) collective-permute-start(bf16[4,20,8,5120]{3,2,1,0:T(8,128)(2,1)} %bitcast_dynamic-update-slice_fusion.6), channel_id=1, source_target_pairs={{0,4},{4,0},{8,12},{12,8},{16,20},{20,16},{24,28},{28,24},{1,5},{5... | collective-permute-start | bytes 19660808 | tf_op jit(solution)/shard_map/ppermute | solution.py:86
  261.6 40.6 %collective-permute-start.13 = (bf16[1280,640]{1,0:T(8,128)(2,1)S(1)}, bf16[1280,640]{1,0:T(8,128)(2,1)S(1)}, u32[]{:S(2)}, u32[]{:S(2)}) collective-permute-start(bf16[1280,640]{1,0:T(8,128)(2,1)S(1)} %collective-permute-done.12), channel_id=1, source_target_pairs={{1,2},{2,1},{5,6},{6,5},{9,10},{10,9},{13,14},{14,13},{17,18},{18,... | collective-permute-start | bytes 4915208 | tf_op jit(solution)/shard_map/ppermute | solution.py:59
  263.8 71.0 %collective-permute-start.16 = (bf16[1280,640]{1,0:T(8,128)(2,1)S(1)}, bf16[1280,640]{1,0:T(8,128)(2,1)S(1)}, u32[]{:S(2)}, u32[]{:S(2)}) collective-permute-start(bf16[1280,640]{1,0:T(8,128)(2,1)S(1)} %collective-permute-done.15), channel_id=1, source_target_pairs={{1,0},{2,3},{5,4},{6,7},{9,8},{10,11},{13,12},{14,15},{17,16},{18,... | collective-permute-start | bytes 4915208 | tf_op jit(solution)/shard_map/ppermute | solution.py:60
  265.1 69.7 %collective-permute-start.22 = (bf16[1280,640]{1,0:T(8,128)(2,1)S(1)}, bf16[1280,640]{1,0:T(8,128)(2,1)S(1)}, u32[]{:S(2)}, u32[]{:S(2)}) collective-permute-start(bf16[1280,640]{1,0:T(8,128)(2,1)S(1)} %collective-permute-done.21), channel_id=1, source_target_pairs={{1,2},{2,1},{5,6},{6,5},{9,10},{10,9},{13,14},{14,13},{17,18},{18,... | collective-permute-start | bytes 4915208 | tf_op jit(solution)/shard_map/ppermute | solution.py:59
  299.6 70.2 %collective-permute-start.5 = (bf16[1280,640]{1,0:T(8,128)(2,1)S(1)}, bf16[1280,640]{1,0:T(8,128)(2,1)S(1)}, u32[]{:S(2)}, u32[]{:S(2)}) collective-permute-start(bf16[1280,640]{1,0:T(8,128)(2,1)S(1)} %collective-permute-done.4), channel_id=1, source_target_pairs={{1,0},{2,3},{5,4},{6,7},{9,8},{10,11},{13,12},{14,15},{17,16},{18,... | collective-permute-start | bytes 4915208 | tf_op jit(solution)/shard_map/ppermute | solution.py:61
  302.2 102.8 %collective-permute-start.14 = (bf16[1280,640]{1,0:T(8,128)(2,1)S(1)}, bf16[1280,640]{1,0:T(8,128)(2,1)S(1)}, u32[]{:S(2)}, u32[]{:S(2)}) collective-permute-start(bf16[1280,640]{1,0:T(8,128)(2,1)S(1)} %collective-permute-done.13), channel_id=1, source_target_pairs={{1,0},{2,3},{5,4},{6,7},{9,8},{10,11},{13,12},{14,15},{17,16},{18,... | collective-permute-start | bytes 4915208 | tf_op jit(solution)/shard_map/ppermute | solution.py:61
  334.7 164.9 %collective-permute-start.17 = (bf16[4,20,8,5120]{3,2,1,0:T(8,128)(2,1)}, bf16[4,20,8,5120]{3,2,1,0:T(8,128)(2,1)}, u32[]{:S(2)}, u32[]{:S(2)}) collective-permute-start(bf16[4,20,8,5120]{3,2,1,0:T(8,128)(2,1)} %bitcast_dynamic-update-slice_fusion.3), channel_id=1, source_target_pairs={{0,4},{4,0},{8,12},{12,8},{16,20},{20,16},{24,28},{28,24},{1,5},{5... | collective-permute-start | bytes 19660808 | tf_op jit(solution)/shard_map/ppermute | solution.py:86
  334.7 105.3 %collective-permute-start.25 = (bf16[1280,640]{1,0:T(8,128)(2,1)S(1)}, bf16[1280,640]{1,0:T(8,128)(2,1)S(1)}, u32[]{:S(2)}, u32[]{:S(2)}) collective-permute-start(bf16[1280,640]{1,0:T(8,128)(2,1)S(1)} %collective-permute-done.24), channel_id=1, source_target_pairs={{1,0},{2,3},{5,4},{6,7},{9,8},{10,11},{13,12},{14,15},{17,16},{18,... | collective-permute-start | bytes 4915208 | tf_op jit(solution)/shard_map/ppermute | solution.py:60
  369.8 101.8 %collective-permute-start.23 = (bf16[1280,640]{1,0:T(8,128)(2,1)S(1)}, bf16[1280,640]{1,0:T(8,128)(2,1)}, u32[]{:S(2)}, u32[]{:S(2)}) collective-permute-start(bf16[1280,640]{1,0:T(8,128)(2,1)S(1)} %collective-permute-done.22), channel_id=1, source_target_pairs={{1,0},{2,3},{5,4},{6,7},{9,8},{10,11},{13,12},{14,15},{17,16},{18,... | collective-permute-start | bytes 4915208 | tf_op jit(solution)/shard_map/ppermute | solution.py:61
  373.8 102.2 %copy-start.6 = (bf16[1280,640]{1,0:T(8,128)(2,1)}, bf16[1280,640]{1,0:T(8,128)(2,1)S(1)}, u32[]{:S(2)}) copy-start(bf16[1280,640]{1,0:T(8,128)(2,1)S(1)} %get-tuple-element.5) | copy-start | bytes 4915204
  404.9 120.6 %collective-permute-start.26 = (bf16[4,20,8,5120]{3,2,1,0:T(8,128)(2,1)}, bf16[4,20,8,5120]{3,2,1,0:T(8,128)(2,1)}, u32[]{:S(2)}, u32[]{:S(2)}) collective-permute-start(bf16[4,20,8,5120]{3,2,1,0:T(8,128)(2,1)} %bitcast_dynamic-update-slice_fusion), channel_id=1, source_target_pairs={{0,4},{4,0},{8,12},{12,8},{16,20},{20,16},{24,28},{28,24},{1,5},{5... | collective-permute-start | bytes 19660808 | tf_op jit(solution)/shard_map/ppermute | solution.py:86
  471.7 15.2 %slice-start.4 = ((s8[6553600]{0:T(1024)(128)(4,1)}), s8[4194304]{0:T(1024)(128)(4,1)S(1)}, s32[]{:S(2)}) async-start(s8[6553600]{0:T(1024)(128)(4,1)} %bitcast.130), calls=%async_computation.4 | async-start | bytes 8388608
  476.0 10.9 %slice-start.5 = ((s8[6553600]{0:T(1024)(128)(4,1)}), s8[2359296]{0:T(1024)(128)(4,1)S(1)}, s32[]{:S(2)}) async-start(s8[6553600]{0:T(1024)(128)(4,1)} %bitcast.130), calls=%async_computation.5 | async-start | bytes 4718592
  499.4 1.9 copy-start.4
  499.4 2.4 copy-start.5
  499.4 2.4 copy-start.8
  499.4 2.4 copy-start.14
  501.8 10.0 %copy-start.10 = (f32[4,20,8]{2,1,0:T(8,128)S(1)}, f32[4,20,8]{2,1,0:T(8,128)}, u32[]{:S(2)}) copy-start(f32[4,20,8]{2,1,0:T(8,128)} %copy.39) | copy-start | bytes 7684
  526.7 10.6 %copy-start.9 = (f32[4,20,8]{2,1,0:T(8,128)S(1)}, f32[4,20,8]{2,1,0:T(8,128)}, u32[]{:S(2)}) copy-start(f32[4,20,8]{2,1,0:T(8,128)} %copy.45) | copy-start | bytes 7684
  (3 other events, 4.3 us)

commit v2 on v0

--- a/solution.py
+++ b/solution.py
@@ -1,6 +1,8 @@
 import jax
 import jax.numpy as jnp
 from jax import lax
+from jax.experimental import pallas as pl
+from jax.experimental.pallas import tpu as pltpu
 from jax.sharding import PartitionSpec as P
 
 VIRG = 160
@@ -52,8 +54,208 @@
     return jnp.stack(results)
 
 
+def kernel(a_ref, b_ref, cycle_ref, all_a, all_b, z_send, z_recv, p_send, p_recv, own_sem):
+    blocks = a_ref.shape[0]
+    pair = lax.axis_index("pair")
+    row = lax.axis_index("row")
+    near = row ^ 1
+    across = 3 - row
+    is_inner = (row == 1) | (row == 2)
+
+    barrier = pltpu.get_barrier_semaphore()
+    friends = [(pair, near), (pair, across)] + [(pair ^ step, row) for step in (1, 2, 4, 6)]
+    for friend in friends:
+        pl.semaphore_signal(
+            barrier, inc=1, device_id=friend, device_id_type=pl.DeviceIdType.MESH
+        )
+    pl.semaphore_wait(barrier, len(friends))
+
+    def z_copy(kind, block):
+        source, slot, target = {
+            "near": (b_ref.at[block], row, near),
+            "mid_own": (b_ref.at[block], row, across),
+            "mid_near": (all_b.at[block, near], near, across),
+            "end_inner": (all_b.at[block, across], across, near),
+            "end_outer": (all_b.at[block, across ^ 1], across ^ 1, near),
+        }[kind]
+        place = ["near", "mid_own", "mid_near", "end_inner", "end_outer"].index(kind)
+        return pltpu.make_async_remote_copy(
+            src_ref=source,
+            dst_ref=all_b.at[block, slot],
+            send_sem=z_send.at[place, block],
+            recv_sem=z_recv.at[place, block],
+            device_id=(pair, target),
+            device_id_type=pl.DeviceIdType.MESH,
+        )
+
+    def plane_copy(step, block):
+        return pltpu.make_async_remote_copy(
+            src_ref=a_ref.at[block],
+            dst_ref=all_a.at[block, pair],
+            send_sem=p_send.at[step - 1, block],
+            recv_sem=p_recv.at[step - 1, block],
+            device_id=(pair ^ (2 * step), row),
+            device_id_type=pl.DeviceIdType.MESH,
+        )
+
+    def core_copy(step, block):
+        piece = pair ^ (2 * step)
+        return pltpu.make_async_remote_copy(
+            src_ref=a_ref.at[block] if step == 0 else all_a.at[block, piece],
+            dst_ref=all_a.at[block, piece],
+            send_sem=p_send.at[3 + step, block],
+            recv_sem=p_recv.at[3 + step, block],
+            device_id=(pair ^ 1, row),
+            device_id_type=pl.DeviceIdType.MESH,
+        )
+
+    def own_copies(block):
+        return [
+            pltpu.make_async_copy(a_ref.at[block], all_a.at[block, pair], own_sem.at[0, block]),
+            pltpu.make_async_copy(b_ref.at[block], all_b.at[block, row], own_sem.at[1, block]),
+        ]
+
+    def plane_start(block):
+        for step in (1, 2, 3):
+            plane_copy(step, block).start()
+        core_copy(0, block).start()
+
+    def plane_forward(block):
+        for step in (1, 2, 3):
+            plane_copy(step, block).wait_recv()
+            core_copy(step, block).start()
+
+    def multiply(block):
+        for copy in own_copies(block):
+            copy.wait()
+        for step in range(4):
+            core_copy(step, block).wait_recv()
+
+        @pl.when(jnp.logical_not(is_inner))
+        def _():
+            z_copy("end_inner", block).wait_recv()
+            z_copy("end_outer", block).wait_recv()
+
+        def tile(a_tile, b_tile, c_tile):
+            rows = a_tile.shape[0] * a_tile.shape[1]
+            depth = b_tile.shape[1]
+
+            def add(part, total):
+                start = pl.multiple_of(part * depth, depth)
+                left = a_tile[:, :, pl.ds(start, depth)].reshape(rows, depth)
+                return total + jnp.dot(left, b_tile[part], preferred_element_type=jnp.float32)
+
+            c_tile[...] = lax.fori_loop(
+                0, b_tile.shape[0], add, jnp.zeros(c_tile.shape, jnp.float32)
+            )
+
+        count, rows, width = all_a.shape[1:]
+        pltpu.emit_pipeline(
+            tile,
+            grid=(count // 2,),
+            in_specs=[
+                pl.BlockSpec((2, rows, width), lambda i: (i, 0, 0)),
+                pl.BlockSpec(all_b.shape[1:], lambda i: (0, 0, 0)),
+            ],
+            out_specs=[pl.BlockSpec((2 * rows, cycle_ref.shape[2]), lambda i: (i, 0))],
+        )(all_a.at[block], all_b.at[block], cycle_ref.at[block])
+
+    z_copy("near", 0).start()
+    plane_start(0)
+
+    @pl.when(is_inner)
+    def _():
+        z_copy("mid_own", 0).start()
+
+    plane_start(1)
+    for block in range(blocks):
+        for copy in own_copies(block):
+            copy.start()
+    for block in range(blocks):
+        z_copy("near", block).wait_recv()
+        if block + 1 < blocks:
+            z_copy("near", block + 1).start()
+
+        @pl.when(is_inner)
+        def _():
+            z_copy("mid_near", block).start()
+            z_copy("mid_own", block).wait_recv()
+            z_copy("end_inner", block).start()
+            if block + 1 < blocks:
+                z_copy("mid_own", block + 1).start()
+            z_copy("mid_near", block).wait_recv()
+            z_copy("end_outer", block).start()
+
+        plane_forward(block)
+        if block + 2 < blocks:
+            plane_start(block + 2)
+        if block >= 1 and block + 1 < blocks:
+            multiply(block - 1)
+    for block in range(max(blocks - 2, 0), blocks):
+        multiply(block)
+    for block in range(blocks):
+        z_copy("near", block).wait_send()
+        for step in (1, 2, 3):
+            plane_copy(step, block).wait_send()
+        for step in range(4):
+            core_copy(step, block).wait_send()
+
+        @pl.when(is_inner)
+        def _():
+            for kind in ("mid_own", "mid_near", "end_inner", "end_outer"):
+                z_copy(kind, block).wait_send()
+
+
+def linked_body(
+    amplitudes,
+    integrals,
+    occupied_irrep,
+    virtual_order,
+    block_irreps,
+    occupied_energy,
+    virtual_energy,
+):
+    blocks, virt_local, occ_local, pair_width = amplitudes.shape
+    depth, column_width = integrals.shape[1:]
+    rows = virt_local * occ_local
+    shift = shift_table(
+        occupied_irrep, virtual_order, block_irreps, occupied_energy, virtual_energy
+    )
+    row_shift = lax.dynamic_slice_in_dim(shift, lax.axis_index("row") * occ_local, occ_local, 2)
+    col_shift = lax.dynamic_slice_in_dim(
+        shift.reshape(blocks, pair_width), lax.axis_index("pair") * column_width, column_width, 1
+    )
+    cycle_term = pl.pallas_call(
+        kernel,
+        out_shape=(
+            jax.ShapeDtypeStruct((blocks, 8 * rows, column_width), jnp.float32),
+            jax.ShapeDtypeStruct((blocks, 8, rows, pair_width), jnp.bfloat16),
+            jax.ShapeDtypeStruct((blocks, 4, depth, column_width), jnp.bfloat16),
+        ),
+        in_specs=[pl.BlockSpec(memory_space=pl.ANY)] * 2,
+        out_specs=(pl.BlockSpec(memory_space=pl.ANY),) * 3,
+        scratch_shapes=[
+            pltpu.SemaphoreType.DMA((5, blocks)),
+            pltpu.SemaphoreType.DMA((5, blocks)),
+            pltpu.SemaphoreType.DMA((7, blocks)),
+            pltpu.SemaphoreType.DMA((7, blocks)),
+            pltpu.SemaphoreType.DMA((2, blocks)),
+        ],
+        compiler_params=pltpu.CompilerParams(
+            collective_id=0, has_side_effects=True, vmem_limit_bytes=50 * 2**20
+        ),
+    )(amplitudes.reshape(blocks, rows, pair_width), integrals)[0]
+    cycle_term = cycle_term.reshape(blocks, 8 * virt_local, occ_local, column_width)
+    return cycle_term / (row_shift[..., None] + col_shift[:, None, None, :])
+
+
 def solution(mesh):
     placed = (P(None, "pair", "row", None), P(None, "row", "pair"), P(), P(), P(), P(), P())
+    linked = mesh.shape["pair"] == 8 and mesh.shape["row"] == 4
     return jax.shard_map(
-        body, mesh=mesh, in_specs=placed, out_specs=P(None, None, "row", "pair"), check_vma=False
-    )
+        linked_body if linked else body,
+        mesh=mesh,
+        in_specs=placed,
+        out_specs=P(None, None, "row", "pair"),
+        check_vma=False,
+    )

time: 626 us -> 357 us (0.57)
  waiting for transfers between devices: 549 us -> 0 us
  Pallas kernels: 0 us -> 345 us
  matrix products: 46.4 us -> 0 us
  between operations: 13.6 us -> 0.1 us
  local copies, waits for them, and re-layouts: 10.8 us -> 0.77 us
    all_gather x6 -> x0, waiting for transfers between devices: 547 us -> none  [the longest x3 324 us: body(): whole_rows = lax.all_gather(integrals[block], 'row', axis=0, tiled=True)]
    pallas_call x0 -> x1, Pallas kernels: none -> 345 us  [linked_body(): pl.pallas_call(kernel, out_shape=(jax.ShapeDtypeStruct((blocks, 8 * rows,...]
    dot_general x3 -> x0, matrix products: 46.4 us -> none  [body(): product = jnp.dot(flat, whole_rows, preferred_element_type=jnp.float32)]
    div x0 -> x1, other arithmetic: none -> 9.01 us  [linked_body(): return cycle_term / (row_shift[..., None] + col_shift[:, None, None, :])]
  transfers between devices with their start and end apart: 6 -> 0, of which waited for: 6 -> 0; matrix products, arithmetic and copies ran while one was open for 6% -> 0% of each run, Pallas kernels for 0% -> 0%
where the time goes in v2:
time: 357 us; the launch traced here: 356 us
  Pallas kernels  345 us (97%)
  other arithmetic  10.3 us (3%)
    pallas_call x1, Pallas kernels, linked_body(): pl.pallas_call(kernel, out_shape=(jax.ShapeDtypeStruct((blocks, 8 * rows,...  345 us
    div x1, other arithmetic, linked_body(): return cycle_term / (row_shift[..., None] + col_shift[:, None, None, :])  9.01 us

profile of v2, /device:TPU:0, one launch (start us, length us, event | category | flops | bytes accessed | tf_op | source)
XLA Modules:
  0.0 356.4 jit_solution(13580121720689149922)
XLA Ops:
  0.0 0.0 copy-start
  0.0 0.0 copy-start.1
  0.0 0.0 copy-start.3
  0.0 0.0 copy-start.4
  0.0 0.0 copy-start.2
  0.0 345.2 %shard_map.73 = (f32[3,1280,640]{2,1,0:T(8,128)}, bf16[3,8,160,5120]{3,2,1,0:T(8,128)(2,1)}, bf16[3,4,1280,640]{3,2,1,0:T(8,128)(2,1)}) custom-call(bf16[3,160,5120]{2,1,0:T(8,128)(2,1)} %bitcast.3, bf16[3,1280,640]{2,1,0:T(8,128)(2,1)} %b_ref.1), custom_call_target="tpu_custom_call" | custom-call | tf_op jit(solution)/shard_map/pallas_call | solution.py:228
  345.2 0.0 copy-done
  345.2 0.0 copy-done.1
  345.3 1.0 select_reduce_fusion
  346.2 0.1 broadcast_in_dim.47
  346.3 0.0 copy-done.3
  346.3 0.0 copy-done.4
  346.3 0.1 broadcast_xor_fusion
  346.4 0.2 select_reduce_fusion.1
  346.6 0.1 copy.9
  346.7 0.2 reduce_sum.22
  346.9 0.0 copy-done.2
  346.9 0.1 sub.20
  347.0 0.1 dynamic-slice.1
  347.1 0.1 dynamic-slice
  347.1 0.1 dynamic-slice_subtract_fusion
  347.2 0.1 copy.8
  347.4 9.0 %bitcast_divide_fusion = f32[3,160,8,640]{3,2,1,0:T(8,128)} fusion(f32[3,1280,640]{2,1,0:T(8,128)} %get-tuple-element.6, f32[3,640]{1,0:T(4,128)S(1)} %dynamic-slice_subtract_fusion.1, f32[3,160,8]{2,1,0:T(8,128)S(1)} %copy.8), kind=kLoop, calls=%fused_computation | loop fusion | flops 4915200 | bytes 19683840 | tf_op jit(solution)/shard_map/div | solution.py:249
  (3 shorter events, 0.0 us)
Async XLA Ops:
  0.0 345.2 %copy-start = (f32[1280]{0:T(1024)S(1)}, f32[1280]{0:T(1024)}, u32[]{:S(2)}) copy-start(f32[1280]{0:T(1024)} %param.13) | copy-start | bytes 15364
  0.0 345.2 %copy-start.1 = (s32[1280]{0:T(1024)S(1)}, s32[1280]{0:T(1024)}, u32[]{:S(2)}) copy-start(s32[1280]{0:T(1024)} %param.10) | copy-start | bytes 15364
  0.0 346.3 %copy-start.3 = (s32[32]{0:T(128)S(1)}, s32[32]{0:T(128)}, u32[]{:S(2)}) copy-start(s32[32]{0:T(128)} %param.9) | copy-start | bytes 388
  0.0 346.3 %copy-start.4 = (s32[3]{0:T(128)S(1)}, s32[3]{0:T(128)}, u32[]{:S(2)}) copy-start(s32[3]{0:T(128)} %param.11) | copy-start | bytes 40
  0.0 346.9 %copy-start.2 = (f32[32]{0:T(128)S(1)}, f32[32]{0:T(128)}, u32[]{:S(2)}) copy-start(f32[32]{0:T(128)} %param.12) | copy-start | bytes 388

commit v3 on v0

--- a/solution.py
+++ b/solution.py
@@ -1,6 +1,8 @@
 import jax
 import jax.numpy as jnp
 from jax import lax
+from jax.experimental import pallas as pl
+from jax.experimental.pallas import tpu as pltpu
 from jax.sharding import PartitionSpec as P
 
 VIRG = 160
@@ -52,8 +54,372 @@
     return jnp.stack(results)
 
 
+HELPED = (1, 2)
+PIECES = ((0, 256), (256, 384))
+
+
+def kernel(
+    a_ref, b_ref, cycle_ref, all_a, all_b, end_a, part_out, part_in,
+    z_send, z_recv, p_send, p_recv, own_sem,
+):
+    blocks, rows, width = a_ref.shape
+    depth = b_ref.shape[1]
+    half = rows // 2
+    pair = lax.axis_index("pair")
+    row = lax.axis_index("row")
+    near = row ^ 1
+    across = 3 - row
+    is_inner = (row == 1) | (row == 2)
+    is_outer = jnp.logical_not(is_inner)
+
+    barrier = pltpu.get_barrier_semaphore()
+    friends = [(pair, near), (pair, across)] + [(pair ^ step, row) for step in (1, 2, 4)]
+    for friend in friends:
+        pl.semaphore_signal(
+            barrier, inc=1, device_id=friend, device_id_type=pl.DeviceIdType.MESH
+        )
+    pl.semaphore_wait(barrier, len(friends))
+
+    kinds = ["near", "mid_own", "mid_near", "end_inner", "end_outer", "end_a", "part"]
+
+    def z_copy(kind, block, piece=None):
+        place = 2 * kinds.index(kind) + (piece or 0)
+        cols = pl.ds(*PIECES[piece]) if piece is not None else slice(None)
+        if kind == "near":
+            source, dest, target = b_ref.at[block], all_b.at[block, row], near
+        elif kind == "mid_own":
+            source, dest = b_ref.at[block, :, cols], all_b.at[block, row, :, cols]
+            target = across
+        elif kind == "mid_near":
+            source = dest = all_b.at[block, near, :, cols]
+            target = across
+        elif kind == "end_inner":
+            source = dest = all_b.at[block, across]
+            target = near
+        elif kind == "end_outer":
+            source = dest = all_b.at[block, across ^ 1]
+            target = near
+        elif kind == "end_a":
+            start = pl.multiple_of(((3 - row) // 3) * depth, depth)
+            source = a_ref.at[block, :, pl.ds(start, width - depth)]
+            dest = end_a.at[HELPED.index(block), pair]
+            target = near
+        else:
+            source = part_out.at[HELPED.index(block), :, cols]
+            dest = part_in.at[HELPED.index(block), :, cols]
+            target = near
+        return pltpu.make_async_remote_copy(
+            src_ref=source,
+            dst_ref=dest,
+            send_sem=z_send.at[place, block],
+            recv_sem=z_recv.at[place, block],
+            device_id=(pair, target),
+            device_id_type=pl.DeviceIdType.MESH,
+        )
+
+    class Gather:
+        def __init__(self, number, own, whole):
+            self.number, self.own, self.whole = number, own, whole
+
+        def copy(self, kind):
+            whole = self.whole
+            top, bottom = pl.ds(0, half), pl.ds(half, half)
+            source, dest, step = [
+                (self.own, whole.at[pair], 2),
+                (self.own, whole.at[pair], 4),
+                (whole.at[pair ^ 4, bottom], whole.at[pair ^ 4, bottom], 2),
+                (whole.at[pair ^ 2, top], whole.at[pair ^ 2, top], 4),
+                (self.own, whole.at[pair], 1),
+                (whole.at[pair ^ 2], whole.at[pair ^ 2], 1),
+                (whole.at[pair ^ 4], whole.at[pair ^ 4], 1),
+                (whole.at[pair ^ 6], whole.at[pair ^ 6], 1),
+            ][kind]
+            return pltpu.make_async_remote_copy(
+                src_ref=source,
+                dst_ref=dest,
+                send_sem=p_send.at[kind, self.number],
+                recv_sem=p_recv.at[kind, self.number],
+                device_id=(pair ^ step, row),
+                device_id_type=pl.DeviceIdType.MESH,
+            )
+
+        def first(self):
+            for kind in (0, 1, 4):
+                self.copy(kind).start()
+
+        def second(self):
+            self.copy(0).wait_recv()
+            self.copy(3).start()
+            self.copy(5).start()
+            self.copy(1).wait_recv()
+            self.copy(2).start()
+            self.copy(6).start()
+
+        def third(self):
+            self.copy(2).wait_recv()
+            self.copy(3).wait_recv()
+            self.copy(7).start()
+
+        def finish(self):
+            for kind in (4, 5, 6, 7):
+                self.copy(kind).wait_recv()
+
+        def drain(self):
+            for kind in range(8):
+                self.copy(kind).wait_send()
+
+    plane = [Gather(block, a_ref.at[block], all_a.at[block]) for block in range(blocks)]
+    ends = [
+        Gather(blocks + spot, end_a.at[spot, pair], end_a.at[spot]) for spot in range(len(HELPED))
+    ]
+
+    def own_copies(block):
+        return [
+            pltpu.make_async_copy(a_ref.at[block], all_a.at[block, pair], own_sem.at[0, block]),
+            pltpu.make_async_copy(b_ref.at[block], all_b.at[block, row], own_sem.at[1, block]),
+        ]
+
+    def chain(a_tile, b_tile, low, high, total):
+        def add(part, total):
+            start = pl.multiple_of(part * depth, depth)
+            left = a_tile[:, :, pl.ds(start, depth)].reshape(-1, depth)
+            return total + jnp.dot(left, b_tile[part], preferred_element_type=jnp.float32)
+
+        return lax.fori_loop(low, high, add, total)
+
+    def help_end(block, piece):
+        spot = HELPED.index(block)
+        z_copy("mid_own", block, piece).wait_recv()
+        z_copy("mid_near", block, piece).wait_recv()
+        if piece == 0:
+            own_copies(block)[1].wait()
+        cols = pl.ds(*PIECES[piece])
+        size = PIECES[piece][1]
+
+        def tile(a_tile, b_tile, c_tile):
+            c_tile[...] = chain(
+                a_tile, b_tile, 0, b_tile.shape[0], jnp.zeros(c_tile.shape, jnp.float32)
+            )
+
+        pltpu.emit_pipeline(
+            tile,
+            grid=(4,),
+            in_specs=[
+                pl.BlockSpec((2, rows, width - depth), lambda i: (i, 0, 0)),
+                pl.BlockSpec((3, depth, size), lambda i: (0, 0, 0)),
+            ],
+            out_specs=[pl.BlockSpec((2 * rows, size), lambda i: (i, 0))],
+        )(
+            end_a.at[spot],
+            all_b.at[block, pl.ds(2 - row, 3), :, cols],
+            part_out.at[spot, :, cols],
+        )
+        z_copy("part", block, piece).start()
+
+    def multiply(block):
+        helped = block in HELPED
+        own_copies(block)[0].wait()
+        plane[block].finish()
+
+        @pl.when(is_outer)
+        def _():
+            own_copies(block)[1].wait()
+            if helped:
+                for piece in range(len(PIECES)):
+                    z_copy("part", block, piece).wait_recv()
+            else:
+                z_copy("end_inner", block).wait_recv()
+                z_copy("end_outer", block).wait_recv()
+
+        if not helped:
+
+            @pl.when(is_inner)
+            def _():
+                own_copies(block)[1].wait()
+
+        low = jnp.where(is_inner, 0, row) if helped else 0
+        high = jnp.where(is_inner, 4, row + 1) if helped else 4
+
+        def tile(a_tile, b_tile, *rest):
+            c_tile = rest[-1]
+            total = jnp.zeros(c_tile.shape, jnp.float32)
+            if helped:
+                total = jnp.where(is_outer, rest[0][...], total)
+            c_tile[...] = chain(a_tile, b_tile, low, high, total)
+
+        square = pl.BlockSpec((2 * rows, cycle_ref.shape[2]), lambda i: (i, 0))
+        extra = [part_in.at[HELPED.index(block)]] if helped else []
+        pltpu.emit_pipeline(
+            tile,
+            grid=(4,),
+            in_specs=[
+                pl.BlockSpec((2, rows, width), lambda i: (i, 0, 0)),
+                pl.BlockSpec(all_b.shape[1:], lambda i: (0, 0, 0)),
+            ]
+            + [square] * len(extra),
+            out_specs=[square],
+        )(all_a.at[block], all_b.at[block], *extra, cycle_ref.at[block])
+
+    both = range(len(PIECES))
+    z_copy("near", 0).start()
+    plane[0].first()
+
+    @pl.when(is_inner)
+    def _():
+        z_copy("mid_own", 0).start()
+
+    for block in range(blocks):
+        for copy in own_copies(block):
+            copy.start()
+    z_copy("near", 0).wait_recv()
+
+    @pl.when(is_outer)
+    def _():
+        z_copy("end_a", 1).start()
+        z_copy("near", 1).start()
+
+    @pl.when(is_inner)
+    def _():
+        z_copy("mid_near", 0).start()
+        z_copy("mid_own", 0).wait_recv()
+        z_copy("end_inner", 0).start()
+        for piece in both:
+            z_copy("mid_own", 1, piece).start()
+
+    plane[0].second()
+
+    @pl.when(is_outer)
+    def _():
+        z_copy("end_a", 1).wait_send()
+        z_copy("end_a", 2).start()
+        z_copy("near", 2).start()
+        plane[1].first()
+
+    @pl.when(is_inner)
+    def _():
+        z_copy("end_a", 1).wait_recv()
+        ends[0].first()
+        z_copy("mid_near", 0).wait_recv()
+        z_copy("end_outer", 0).start()
+        z_copy("near", 1).wait_recv()
+        for piece in both:
+            z_copy("mid_near", 1, piece).start()
+        for piece in both:
+            z_copy("mid_own", 2, piece).start()
+        ends[0].second()
+        plane[1].first()
+
+    plane[0].third()
+
+    @pl.when(is_inner)
+    def _():
+        ends[0].third()
+        z_copy("end_a", 2).wait_recv()
+        ends[1].first()
+        ends[0].finish()
+        help_end(1, 0)
+        help_end(1, 1)
+        z_copy("near", 2).wait_recv()
+        for piece in both:
+            z_copy("mid_near", 2, piece).start()
+        ends[1].second()
+
+    plane[1].second()
+    plane[2].first()
+
+    @pl.when(is_inner)
+    def _():
+        ends[1].third()
+
+    plane[1].third()
+    multiply(0)
+
+    @pl.when(is_inner)
+    def _():
+        ends[1].finish()
+        help_end(2, 0)
+        help_end(2, 1)
+
+    plane[2].second()
+    plane[2].third()
+    multiply(1)
+    multiply(2)
+
+    for gather in plane:
+        gather.drain()
+    z_copy("near", 0).wait_send()
+
+    @pl.when(is_outer)
+    def _():
+        z_copy("near", 1).wait_send()
+        z_copy("near", 2).wait_send()
+        z_copy("end_a", 2).wait_send()
+
+    @pl.when(is_inner)
+    def _():
+        for gather in ends:
+            gather.drain()
+        for kind in ("mid_own", "mid_near", "end_inner", "end_outer"):
+            z_copy(kind, 0).wait_send()
+        for block in HELPED:
+            for piece in both:
+                for kind in ("mid_own", "mid_near", "part"):
+                    z_copy(kind, block, piece).wait_send()
+
+
+def linked_body(
+    amplitudes,
+    integrals,
+    occupied_irrep,
+    virtual_order,
+    block_irreps,
+    occupied_energy,
+    virtual_energy,
+):
+    blocks, virt_local, occ_local, pair_width = amplitudes.shape
+    depth, column_width = integrals.shape[1:]
+    rows = virt_local * occ_local
+    shift = shift_table(
+        occupied_irrep, virtual_order, block_irreps, occupied_energy, virtual_energy
+    )
+    row_shift = lax.dynamic_slice_in_dim(shift, lax.axis_index("row") * occ_local, occ_local, 2)
+    col_shift = lax.dynamic_slice_in_dim(
+        shift.reshape(blocks, pair_width), lax.axis_index("pair") * column_width, column_width, 1
+    )
+    cycle_term = pl.pallas_call(
+        kernel,
+        out_shape=(
+            jax.ShapeDtypeStruct((blocks, 8 * rows, column_width), jnp.float32),
+            jax.ShapeDtypeStruct((blocks, 8, rows, pair_width), jnp.bfloat16),
+            jax.ShapeDtypeStruct((blocks, 4, depth, column_width), jnp.bfloat16),
+            jax.ShapeDtypeStruct((2, 8, rows, pair_width - depth), jnp.bfloat16),
+            jax.ShapeDtypeStruct((2, 8 * rows, column_width), jnp.float32),
+            jax.ShapeDtypeStruct((2, 8 * rows, column_width), jnp.float32),
+        ),
+        in_specs=[pl.BlockSpec(memory_space=pl.ANY)] * 2,
+        out_specs=(pl.BlockSpec(memory_space=pl.ANY),) * 6,
+        scratch_shapes=[
+            pltpu.SemaphoreType.DMA((14, blocks)),
+            pltpu.SemaphoreType.DMA((14, blocks)),
+            pltpu.SemaphoreType.DMA((8, blocks + 2)),
+            pltpu.SemaphoreType.DMA((8, blocks + 2)),
+            pltpu.SemaphoreType.DMA((2, blocks)),
+        ],
+        compiler_params=pltpu.CompilerParams(
+            collective_id=0, has_side_effects=True, vmem_limit_bytes=50 * 2**20
+        ),
+    )(amplitudes.reshape(blocks, rows, pair_width), integrals)[0]
+    cycle_term = cycle_term.reshape(blocks, 8 * virt_local, occ_local, column_width)
+    return cycle_term / (row_shift[..., None] + col_shift[:, None, None, :])
+
+
 def solution(mesh):
     placed = (P(None, "pair", "row", None), P(None, "row", "pair"), P(), P(), P(), P(), P())
+    linked = mesh.shape["pair"] == 8 and mesh.shape["row"] == 4
     return jax.shard_map(
-        body, mesh=mesh, in_specs=placed, out_specs=P(None, None, "row", "pair"), check_vma=False
+        linked_body if linked else body,
+        mesh=mesh,
+        in_specs=placed,
+        out_specs=P(None, None, "row", "pair"),
+        check_vma=False,
     )

time: 626 us -> 410 us (0.65)
  waiting for transfers between devices: 549 us -> 0 us
  Pallas kernels: 0 us -> 398 us
  matrix products: 46.4 us -> 0 us
  between operations: 13.6 us -> 0.1 us
  local copies, waits for them, and re-layouts: 10.8 us -> 0.77 us
    all_gather x6 -> x0, waiting for transfers between devices: 547 us -> none  [the longest x3 324 us: body(): whole_rows = lax.all_gather(integrals[block], 'row', axis=0, tiled=True)]
    pallas_call x0 -> x1, Pallas kernels: none -> 398 us  [linked_body(): pl.pallas_call(kernel, out_shape=(jax.ShapeDtypeStruct((blocks, 8 * rows,...]
    dot_general x3 -> x0, matrix products: 46.4 us -> none  [body(): product = jnp.dot(flat, whole_rows, preferred_element_type=jnp.float32)]
    div x0 -> x1, other arithmetic: none -> 9.01 us  [linked_body(): return cycle_term / (row_shift[..., None] + col_shift[:, None, None, :])]
  transfers between devices with their start and end apart: 6 -> 0, of which waited for: 6 -> 0; matrix products, arithmetic and copies ran while one was open for 6% -> 0% of each run, Pallas kernels for 0% -> 0%
where the time goes in v3:
time: 410 us; the launch traced here: 409 us
  Pallas kernels  398 us (97%)
  other arithmetic  10.3 us (3%)
    pallas_call x1, Pallas kernels, linked_body(): pl.pallas_call(kernel, out_shape=(jax.ShapeDtypeStruct((blocks, 8 * rows,...  398 us
    div x1, other arithmetic, linked_body(): return cycle_term / (row_shift[..., None] + col_shift[:, None, None, :])  9.01 us

profile of v3, /device:TPU:0, one launch (start us, length us, event | category | flops | bytes accessed | tf_op | source)
XLA Modules:
  0.0 409.2 jit_solution(2352842628951872513)
XLA Ops:
  0.0 0.0 copy-start
  0.0 0.0 copy-start.1
  0.0 0.0 copy-start.3
  0.0 0.0 copy-start.4
  0.0 0.0 copy-start.2
  0.0 398.1 %shard_map.73 = (f32[3,1280,640]{2,1,0:T(8,128)}, bf16[3,8,160,5120]{3,2,1,0:T(8,128)(2,1)}, bf16[3,4,1280,640]{3,2,1,0:T(8,128)(2,1)}, bf16[2,8,160,3840]{3,2,1...) custom-call(bf16[3,160,5120]{2,1,0:T(8,128)(2,1)} %bitcast.3, bf16[3,1280,640]{2,1,0:T(8,128)(2,1)} %b_ref.1), custom_call_target="tpu_custom_call" | custom-call | tf_op jit(solution)/shard_map/pallas_call | solution.py:389
  398.1 0.0 copy-done
  398.1 0.0 copy-done.1
  398.1 1.0 select_reduce_fusion
  399.0 0.1 broadcast_in_dim.47
  399.1 0.0 copy-done.3
  399.1 0.0 copy-done.4
  399.1 0.1 broadcast_xor_fusion
  399.2 0.2 select_reduce_fusion.1
  399.4 0.1 copy.9
  399.5 0.2 reduce_sum.22
  399.7 0.0 copy-done.2
  399.7 0.1 sub.20
  399.8 0.1 dynamic-slice.1
  399.9 0.1 dynamic-slice
  400.0 0.1 dynamic-slice_subtract_fusion
  400.1 0.1 copy.8
  400.2 9.0 %bitcast_divide_fusion = f32[3,160,8,640]{3,2,1,0:T(8,128)} fusion(f32[3,1280,640]{2,1,0:T(8,128)} %get-tuple-element.6, f32[3,640]{1,0:T(4,128)S(1)} %dynamic-slice_subtract_fusion.1, f32[3,160,8]{2,1,0:T(8,128)S(1)} %copy.8), kind=kLoop, calls=%fused_computation | loop fusion | flops 4915200 | bytes 19683840 | tf_op jit(solution)/shard_map/div | solution.py:413
  (3 shorter events, 0.0 us)
Async XLA Ops:
  0.0 398.1 %copy-start = (f32[1280]{0:T(1024)S(1)}, f32[1280]{0:T(1024)}, u32[]{:S(2)}) copy-start(f32[1280]{0:T(1024)} %param.13) | copy-start | bytes 15364
  0.0 398.1 %copy-start.1 = (s32[1280]{0:T(1024)S(1)}, s32[1280]{0:T(1024)}, u32[]{:S(2)}) copy-start(s32[1280]{0:T(1024)} %param.10) | copy-start | bytes 15364
  0.0 399.1 %copy-start.3 = (s32[32]{0:T(128)S(1)}, s32[32]{0:T(128)}, u32[]{:S(2)}) copy-start(s32[32]{0:T(128)} %param.9) | copy-start | bytes 388
  0.0 399.1 %copy-start.4 = (s32[3]{0:T(128)S(1)}, s32[3]{0:T(128)}, u32[]{:S(2)}) copy-start(s32[3]{0:T(128)} %param.11) | copy-start | bytes 40
  0.0 399.7 %copy-start.2 = (f32[32]{0:T(128)S(1)}, f32[32]{0:T(128)}, u32[]{:S(2)}) copy-start(f32[32]{0:T(128)} %param.12) | copy-start | bytes 388

commit v4 on v2

--- a/solution.py
+++ b/solution.py
@@ -54,7 +54,7 @@
     return jnp.stack(results)
 
 
-def kernel(a_ref, b_ref, cycle_ref, all_a, all_b, z_send, z_recv, p_send, p_recv, own_sem):
+def kernel(a_ref, b_ref, cycle_ref, all_a, all_b, partial, z_send, z_recv, p_send, p_recv, own_sem):
     blocks = a_ref.shape[0]
     pair = lax.axis_index("pair")
     row = lax.axis_index("row")
@@ -125,7 +125,7 @@
             plane_copy(step, block).wait_recv()
             core_copy(step, block).start()
 
-    def multiply(block):
+    def arrived(block):
         for copy in own_copies(block):
             copy.wait()
         for step in range(4):
@@ -134,31 +134,42 @@
         @pl.when(jnp.logical_not(is_inner))
         def _():
             z_copy("end_inner", block).wait_recv()
+
+    def last_arrived(block):
+        @pl.when(jnp.logical_not(is_inner))
+        def _():
             z_copy("end_outer", block).wait_recv()
 
-        def tile(a_tile, b_tile, c_tile):
-            rows = a_tile.shape[0] * a_tile.shape[1]
-            depth = b_tile.shape[1]
-
+    def multiply(block, first, parts, goal, extra=()):
+        count, rows, _ = all_a.shape[1:]
+        depth, columns = all_b.shape[2:]
+
+        def tile(a_tile, b_tile, *rest):
             def add(part, total):
                 start = pl.multiple_of(part * depth, depth)
-                left = a_tile[:, :, pl.ds(start, depth)].reshape(rows, depth)
+                left = a_tile[:, :, pl.ds(start, depth)].reshape(2 * rows, depth)
                 return total + jnp.dot(left, b_tile[part], preferred_element_type=jnp.float32)
 
-            c_tile[...] = lax.fori_loop(
-                0, b_tile.shape[0], add, jnp.zeros(c_tile.shape, jnp.float32)
-            )
-
-        count, rows, width = all_a.shape[1:]
+            begin = rest[0][...] if extra else jnp.zeros(rest[-1].shape, jnp.float32)
+            rest[-1][...] = lax.fori_loop(0, parts, add, begin)
+
+        square = pl.BlockSpec((2 * rows, columns), lambda i: (i, 0))
+        start = pl.multiple_of(first * depth, depth)
         pltpu.emit_pipeline(
             tile,
             grid=(count // 2,),
             in_specs=[
-                pl.BlockSpec((2, rows, width), lambda i: (i, 0, 0)),
-                pl.BlockSpec(all_b.shape[1:], lambda i: (0, 0, 0)),
-            ],
-            out_specs=[pl.BlockSpec((2 * rows, cycle_ref.shape[2]), lambda i: (i, 0))],
-        )(all_a.at[block], all_b.at[block], cycle_ref.at[block])
+                pl.BlockSpec((2, rows, parts * depth), lambda i: (i, 0, 0)),
+                pl.BlockSpec((parts, depth, columns), lambda i: (0, 0, 0)),
+            ]
+            + [square] * len(extra),
+            out_specs=[square],
+        )(
+            all_a.at[block, :, :, pl.ds(start, parts * depth)],
+            all_b.at[block, pl.ds(first, parts)],
+            *extra,
+            goal,
+        )
 
     z_copy("near", 0).start()
     plane_start(0)
@@ -190,9 +201,16 @@
         if block + 2 < blocks:
             plane_start(block + 2)
         if block >= 1 and block + 1 < blocks:
-            multiply(block - 1)
-    for block in range(max(blocks - 2, 0), blocks):
-        multiply(block)
+            arrived(block - 1)
+            last_arrived(block - 1)
+            multiply(block - 1, 0, 4, cycle_ref.at[block - 1])
+    arrived(blocks - 2)
+    last_arrived(blocks - 2)
+    multiply(blocks - 2, 0, 4, cycle_ref.at[blocks - 2])
+    arrived(blocks - 1)
+    multiply(blocks - 1, row // 2, 3, partial)
+    last_arrived(blocks - 1)
+    multiply(blocks - 1, 3 * (1 - row // 2), 1, cycle_ref.at[blocks - 1], (partial,))
     for block in range(blocks):
         z_copy("near", block).wait_send()
         for step in (1, 2, 3):
@@ -231,9 +249,10 @@
             jax.ShapeDtypeStruct((blocks, 8 * rows, column_width), jnp.float32),
             jax.ShapeDtypeStruct((blocks, 8, rows, pair_width), jnp.bfloat16),
             jax.ShapeDtypeStruct((blocks, 4, depth, column_width), jnp.bfloat16),
+            jax.ShapeDtypeStruct((8 * rows, column_width), jnp.float32),
         ),
         in_specs=[pl.BlockSpec(memory_space=pl.ANY)] * 2,
-        out_specs=(pl.BlockSpec(memory_space=pl.ANY),) * 3,
+        out_specs=(pl.BlockSpec(memory_space=pl.ANY),) * 4,
         scratch_shapes=[
             pltpu.SemaphoreType.DMA((5, blocks)),
             pltpu.SemaphoreType.DMA((5, blocks)),

time: 357 us -> 344 us (0.964)
  Pallas kernels: 345 us -> 333 us
    pallas_call x1, Pallas kernels: 345 us -> 333 us  [linked_body(): pl.pallas_call(kernel, out_shape=(jax.ShapeDtypeStruct((blocks, 8 * rows,...]
where the time goes in v4:
time: 344 us
  Pallas kernels  333 us (97%)
  other arithmetic  10.3 us (3%)
    pallas_call x1, Pallas kernels, linked_body(): pl.pallas_call(kernel, out_shape=(jax.ShapeDtypeStruct((blocks, 8 * rows,...  333 us
    div x1, other arithmetic, linked_body(): return cycle_term / (row_shift[..., None] + col_shift[:, None, None, :])  9.01 us

profile of v4, /device:TPU:0, one launch (start us, length us, event | category | flops | bytes accessed | tf_op | source)
XLA Modules:
  0.0 343.9 jit_solution(6705169642847558937)
XLA Ops:
  0.0 0.0 copy-start
  0.0 0.0 copy-start.1
  0.0 0.0 copy-start.3
  0.0 0.0 copy-start.4
  0.0 0.0 copy-start.2
  0.0 332.8 %shard_map.73 = (f32[3,1280,640]{2,1,0:T(8,128)}, bf16[3,8,160,5120]{3,2,1,0:T(8,128)(2,1)}, bf16[3,4,1280,640]{3,2,1,0:T(8,128)(2,1)}, f32[1280,640]{1,0:T(8,128)}) custom-call(bf16[3,160,5120]{2,1,0:T(8,128)(2,1)} %bitcast.3, bf16[3,1280,640]{2,1,0:T(8,128)(2,1)} %b_ref.1), custom_call_target="tpu_custom_call" | custom-call | tf_op jit(solution)/shard_map/pallas_call | solution.py:246
  332.8 0.0 copy-done
  332.8 0.0 copy-done.1
  332.8 1.0 select_reduce_fusion
  333.8 0.1 broadcast_in_dim.47
  333.8 0.0 copy-done.3
  333.8 0.0 copy-done.4
  333.8 0.1 broadcast_xor_fusion
  333.9 0.2 select_reduce_fusion.1
  334.1 0.1 copy.9
  334.2 0.2 reduce_sum.22
  334.4 0.0 copy-done.2
  334.4 0.1 sub.20
  334.5 0.1 dynamic-slice.1
  334.6 0.1 dynamic-slice
  334.7 0.1 dynamic-slice_subtract_fusion
  334.8 0.1 copy.8
  334.9 9.0 %bitcast_divide_fusion = f32[3,160,8,640]{3,2,1,0:T(8,128)} fusion(f32[3,1280,640]{2,1,0:T(8,128)} %get-tuple-element.6, f32[3,640]{1,0:T(4,128)S(1)} %dynamic-slice_subtract_fusion.1, f32[3,160,8]{2,1,0:T(8,128)S(1)} %copy.8), kind=kLoop, calls=%fused_computation | loop fusion | flops 4915200 | bytes 19683840 | tf_op jit(solution)/shard_map/div | solution.py:268
  (3 shorter events, 0.0 us)
Async XLA Ops:
  0.0 332.8 %copy-start = (f32[1280]{0:T(1024)S(1)}, f32[1280]{0:T(1024)}, u32[]{:S(2)}) copy-start(f32[1280]{0:T(1024)} %param.13) | copy-start | bytes 15364
  0.0 332.8 %copy-start.1 = (s32[1280]{0:T(1024)S(1)}, s32[1280]{0:T(1024)}, u32[]{:S(2)}) copy-start(s32[1280]{0:T(1024)} %param.10) | copy-start | bytes 15364
  0.0 333.8 %copy-start.3 = (s32[32]{0:T(128)S(1)}, s32[32]{0:T(128)}, u32[]{:S(2)}) copy-start(s32[32]{0:T(128)} %param.9) | copy-start | bytes 388
  0.0 333.8 %copy-start.4 = (s32[3]{0:T(128)S(1)}, s32[3]{0:T(128)}, u32[]{:S(2)}) copy-start(s32[3]{0:T(128)} %param.11) | copy-start | bytes 40
  0.0 334.4 %copy-start.2 = (f32[32]{0:T(128)S(1)}, f32[32]{0:T(128)}, u32[]{:S(2)}) copy-start(f32[32]{0:T(128)} %param.12) | copy-start | bytes 388
